TPU v7x, 256 devices: a whole 4x4x8 slice. The times are simulated.
256 devices in a mesh: row: 16 (over y, z_hi), col: 8 (over x, core), gz: 2 (over z_lo).
Axes of the slice: x: 4, y: 4, z: 8 (z_hi: 4, z_lo: 2; z = z_hi * 2 + z_lo), core: 2. Of those that a mesh axis runs over, the one named last changes fastest.
Arguments:
- source: float32 [2, 4, 1024, 1024], P(None, 'gz', 'row', 'col'), may hold values from -24 to 24
- cell_class: int32 [4, 1024, 1024], P('gz', 'row', 'col'), may hold values from 0 to 7
- coeff_table: float32 [8], replicated, may hold values from 0.5 to 8
- owner_cell: int32 [32768], P(('row', 'col', 'gz')), may hold values from 0 to 16383
- node_pos: float32 [3, 32768], P(None, ('row', 'col', 'gz')), may hold values from 0 to 1
- node_weight: float32 [32768], P(('row', 'col', 'gz')), may hold values from 0.002 to 0.02
Outputs:
- potential: float32 [2, 4, 1024, 1024], P(None, 'gz', 'row', 'col')
- boundary_values: float32 [2, 32768], P(None, ('row', 'col', 'gz'))
Inputs may be any that keep to these rules, and one draw needn't show every extreme that they name: `owner_cell`: each boundary node names a cell of its own device's tile, a flat index over 2 x 64 x 128 cells with the layer slowest.
All inputs are finite; a program needn't handle non-finite values.
Results may differ from a plain program's by a relative error of at most 0.0003.
Values sent between devices are 32-bit elements; how exact they have to be, the bound alone decides.
No kernel may reach another device: no remote copies, remote signals or barrier semaphores. Data moves between devices by JAX's collectives and lax.ppermute only.
A program may use at most 64 MiB of HBM per device.

v0:
```python
import jax
import jax.numpy as jnp
from jax import lax
from jax.sharding import PartitionSpec as P

SWEEPS = 4
OMEGA = 0.8
RELAX = 0.5
SOFTEN = 0.01


def extended(shard, sides, width):
    for axis, dim in sides:
        size, length = (lax.axis_size(axis), shard.shape[dim])
        up = [(i, (i + 1) % size) for i in range(size - 1)]
        down = [(j, i) for i, j in up]
        last = lax.slice_in_dim(shard, length - width, length, axis=dim)
        leading = lax.slice_in_dim(shard, 0, width, axis=dim)
        before = lax.ppermute(last, axis, up)
        after = lax.ppermute(leading, axis, down)
        shard = jnp.concatenate([before, shard, after], axis=dim)
    return shard


def lookup_diagonal(cell_class, coeff_table):
    summed = jnp.zeros(cell_class.shape, jnp.float32)
    for class_level in range(coeff_table.shape[0]):
        summed = summed + jnp.where(
            cell_class == class_level, coeff_table[class_level], jnp.zeros((), coeff_table.dtype)
        )
    return 6.0 + summed


def stencil_update(padded, field, forcing, diagonal):
    beside = padded[:, 2:, 1:-1, 1:-1] + padded[:, :-2, 1:-1, 1:-1]
    beside = beside + padded[:, 1:-1, 2:, 1:-1] + padded[:, 1:-1, :-2, 1:-1]
    beside = beside + padded[:, 1:-1, 1:-1, 2:] + padded[:, 1:-1, 1:-1, :-2]
    return field + OMEGA * (forcing - (diagonal * field - beside)) / diagonal


def sweep_once(field, forcing, diagonal):
    padded = extended(field, (("row", 2), ("col", 3), ("gz", 1)), 1)
    return stencil_update(padded, field, forcing, diagonal)


def on_device(source, cell_class, coeff_table, owner_cell, node_pos, node_weight):
    images, depth, rows_x, cols_y = source.shape
    cell_count = depth * rows_x * cols_y
    node_count = owner_cell.shape[0]
    diagonal = lookup_diagonal(cell_class, coeff_table)

    def relax_all(field, forcing):
        for repeat in range(SWEEPS):
            field = sweep_once(field, forcing, diagonal)
        return field

    target_pos = lax.all_gather(node_pos, ("col", "gz"), axis=1, tiled=True)
    source_meta = lax.all_gather(
        jnp.concatenate([node_pos, node_weight[None, :]], 0), "row", axis=1, tiled=True
    )
    target_count = target_pos.shape[1]
    block_rows = min(512, target_count)
    target_blocks = target_pos.reshape(3, target_count // block_rows, block_rows).transpose(1, 0, 2)

    def kernel_apply(piece_traces):

        def block_sum(target):
            diff_x = target[0][:, None] - source_meta[0][None, :]
            diff_y = target[1][:, None] - source_meta[1][None, :]
            diff_z = target[2][:, None] - source_meta[2][None, :]
            inverse = lax.rsqrt(diff_x * diff_x + diff_y * diff_y + diff_z * diff_z + SOFTEN)
            kernel = source_meta[3][None, :] * diff_z * inverse * inverse * inverse
            return lax.dot_general(
                piece_traces,
                kernel,
                (((1,), (1,)), ((), ())),
                precision=lax.Precision.HIGHEST,
                preferred_element_type=jnp.float32,
            )

        pieces = lax.map(block_sum, target_blocks)
        return pieces.transpose(1, 0, 2).reshape(images, target_count)

    def fk_round(forcing, first, second):
        first = relax_all(first, forcing)
        trace = jnp.take(first.reshape(images, cell_count), owner_cell, axis=1)
        partial_sums = kernel_apply(lax.all_gather(trace, "row", axis=1, tiled=True))
        whole_sums = lax.psum(partial_sums, ("col", "gz"))
        summed = lax.dynamic_slice_in_dim(
            whole_sums, lax.axis_index(("col", "gz")) * node_count, node_count, 1
        )
        values = -0.5 * trace + summed
        spread = (
            jnp.zeros((images, cell_count), jnp.float32)
            .at[:, owner_cell]
            .add(values)
            .reshape(source.shape)
        )
        second = relax_all(second, spread)
        return (first, second, values)

    first = jnp.zeros(source.shape, jnp.float32)
    second = jnp.zeros(source.shape, jnp.float32)
    first, second, values = fk_round(source, first, second)
    forcing = source - RELAX * (first + second)
    first, second, values = fk_round(forcing, first, second)
    return (first + second, values)


def solution(mesh):
    return jax.shard_map(
        on_device,
        mesh=mesh,
        in_specs=(
            P(None, "gz", "row", "col"),
            P("gz", "row", "col"),
            P(),
            P(("row", "col", "gz")),
            P(None, ("row", "col", "gz")),
            P(("row", "col", "gz")),
        ),
        out_specs=(P(None, "gz", "row", "col"), P(None, ("row", "col", "gz"))),
        check_vma=False,
    )
```

profile of v0, /device:TPU:1, one launch (start us, length us, event | category | flops | bytes accessed | tf_op | source)
XLA Modules:
  0.0 793.1 jit_solution(11103989547739344262)
XLA Ops:
  0.7 5.8 collective-permute-start
  7.8 5.8 collective-permute-done.1
  30.7 6.0 broadcast_multiply_fusion
  37.9 5.7 collective-permute-start.6
  75.6 5.4 collective-permute-start.14
  93.1 33.6 %all_gather.12 = f32[4,2048]{1,0:T(4,128)S(1)} all-gather(f32[4,128]{1,0:T(4,128)S(1)} %pad_maximum_fusion.298), channel_id=1, replica_groups=mesh['row'=16,'col'=8,'gz'=2] {'row'}, dimensions={1}, use_global_device_ids=true | all-gather | bytes 34816 | tf_op jit(solution)/shard_map/all_gather | solution.py:58
  130.1 29.4 %all_gather.13 = f32[3,2048]{1,0:T(4,128)S(1)} all-gather(f32[3,128]{1,0:T(4,128)S(1)} %copy-done.1), channel_id=1, replica_groups=mesh['row'=16,'col'=8,'gz'=2] {'col','gz'}, dimensions={1}, use_global_device_ids=true | all-gather | bytes 26112 | tf_op jit(solution)/shard_map/all_gather | solution.py:57
  184.9 50.7 %all_gather.14 = f32[2,2048]{0,1:T(8,128)S(1)} all-gather(f32[2,128]{0,1:T(8,128)S(1)} %select_bitcast_fusion.1), channel_id=1, replica_groups=mesh['row'=16,'col'=8,'gz'=2] {'row'}, dimensions={1}, use_global_device_ids=true | all-gather | bytes 17408 | tf_op jit(solution)/shard_map/all_gather | solution.py:87
  236.0 22.4 %while.20 = (s32[]{:T(128)}, f32[4,2,512]{2,1,0:T(2,128)S(1)}, f32[4,2048]{1,0:T(4,128)S(1)}, f32[4,3,512]{2,1,0:T(4,128)S(1)}, f32[2,2048]{1,0:T(2,128)S(1)}, /*index=5*/s32[]{:T(128)}, s32[]{:T(128)}, s32[]{}, s32[]{}) while((s32[]{:T(128)}, f32[4,2,512]{2,1,0:T(2,128)S(1)}, f32[4,2048]{1,0:T(4,128)S(1)}, f32[4,3,512]{2,1,0:T(4,128)S(1)}, ...), condition=%wide.region_1.3_spmd, body=%wide.region_0.2_spmd.sunk | while | flops 38797316 | bytes 137349 | solution.py:81
  236.0 5.5 fusion.246
  241.6 5.5 fusion.246
  247.2 5.5 fusion.246
  252.8 5.5 fusion.246
  258.8 80.7 %psum.14 = f32[2,2048]{0,1:T(8,128)S(1)} all-reduce(f32[2,2048]{0,1:T(8,128)S(1)} %bitcast.103), channel_id=1, replica_groups=mesh['row'=16,'col'=8,'gz'=2] {'col','gz'}, use_global_device_ids=true, to_apply=%region_2.4 | all-reduce | flops 4096 | bytes 32768 | tf_op jit(solution)/shard_map/psum | solution.py:88
  344.4 5.2 copy.11
  349.6 6.2 collective-permute-start.24
  363.1 5.3 collective-permute-start.27
  442.3 5.7 collective-permute-start.48
  453.4 8.3 %collective-permute-start.50 = (f32[2,2,66,1]{3,2,1,0:T(8,128)S(1)}, f32[2,2,66,1]{3,2,1,0:T(8,128)S(1)}, u32[]{:S(2)}, u32[]{:S(2)}) collective-permute-start(f32[2,2,66,1]{3,2,1,0:T(8,128)S(1)} %get-tuple-element.155), channel_id=1, source_target_pairs={{0,2},{2,4},{4,6},{6,8},{8,10},{10,12},{12,14},{1,3},{3,5},{5,7},{... | collective-permute-start | bytes 3176 | tf_op jit(solution)/shard_map/ppermute | solution.py:19
  491.8 5.7 collective-permute-start.66
  513.2 5.7 collective-permute-start.68
  551.2 45.3 %all_gather.15 = f32[2,2048]{0,1:T(8,128)S(1)} all-gather(f32[2,128]{0,1:T(8,128)S(1)} %select_bitcast_fusion), channel_id=1, replica_groups=mesh['row'=16,'col'=8,'gz'=2] {'row'}, dimensions={1}, use_global_device_ids=true | all-gather | bytes 17408 | tf_op jit(solution)/shard_map/all_gather | solution.py:87
  596.9 22.4 %while.21 = (s32[]{:T(128)}, f32[4,2,512]{2,1,0:T(2,128)S(1)}, f32[4,2048]{1,0:T(4,128)S(1)}, f32[4,3,512]{2,1,0:T(4,128)S(1)}, f32[2,2048]{1,0:T(2,128)S(1)}, /*index=5*/s32[]{:T(128)}, s32[]{:T(128)}, s32[]{}, s32[]{}) while((s32[]{:T(128)}, f32[4,2,512]{2,1,0:T(2,128)S(1)}, f32[4,2048]{1,0:T(4,128)S(1)}, f32[4,3,512]{2,1,0:T(4,128)S(1)}, ...), condition=%wide.region_5.7_spmd, body=%wide.region_4.6_spmd.sunk | while | flops 38797316 | bytes 137349 | solution.py:81
  596.9 5.5 fusion.249
  602.5 5.5 fusion.249
  608.1 5.5 fusion.249
  613.7 5.5 fusion.249
  619.6 77.1 %psum.15 = f32[2,2048]{0,1:T(8,128)S(1)} all-reduce(f32[2,2048]{0,1:T(8,128)S(1)} %bitcast.104), channel_id=1, replica_groups=mesh['row'=16,'col'=8,'gz'=2] {'col','gz'}, use_global_device_ids=true, to_apply=%region_6.8 | all-reduce | flops 4096 | bytes 32768 | tf_op jit(solution)/shard_map/psum | solution.py:88
  701.7 5.2 copy.18
  718.6 5.2 collective-permute-start.75
  744.1 5.6 collective-permute-start.80
  772.4 5.6 collective-permute-start.86
  (303 shorter events, 336.9 us)
Async XLA Ops:
  13.8 8.5 %collective-permute-start.2 = (f32[2,2,66,1]{3,2,1,0:T(8,128)S(1)}, f32[2,2,66,1]{3,2,1,0:T(8,128)S(1)}, u32[]{:S(2)}, u32[]{:S(2)}) collective-permute-start(f32[2,2,66,1]{3,2,1,0:T(8,128)S(1)} %get-tuple-element.171), channel_id=1, source_target_pairs={{0,2},{2,4},{4,6},{6,8},{8,10},{10,12},{12,14},{1,3},{3,5},{5,7},{... | collective-permute-start | bytes 3176 | tf_op jit(solution)/shard_map/ppermute | solution.py:19
  25.4 11.3 %collective-permute-start.4 = (f32[2,1,66,130]{3,2,1,0:T(8,128)S(1)}, f32[2,1,66,130]{3,2,1,0:T(8,128)S(1)}, u32[]{:S(2)}, u32[]{:S(2)}) collective-permute-start(f32[2,1,66,130]{3,2,1,0:T(8,128)S(1)} %get-tuple-element.140), channel_id=1, source_target_pairs={{1,0},{3,2},{5,4},{7,6},{9,8},{11,10},{13,12},{15,14},{17,16},{19,... | collective-permute-start | bytes 205928 | tf_op jit(solution)/shard_map/ppermute | solution.py:20
  26.7 10.0 %collective-permute-start.5 = (f32[2,1,66,130]{3,2,1,0:T(8,128)S(1)}, f32[2,1,66,130]{3,2,1,0:T(8,128)S(1)}, u32[]{:S(2)}, u32[]{:S(2)}) collective-permute-start(f32[2,1,66,130]{3,2,1,0:T(8,128)S(1)} %get-tuple-element.141), channel_id=1, source_target_pairs={{0,1},{2,3},{4,5},{6,7},{8,9},{10,11},{12,13},{14,15},{16,17},{18,... | collective-permute-start | bytes 205928 | tf_op jit(solution)/shard_map/ppermute | solution.py:19
  87.7 39.0 %collective-permute-start.16 = (f32[2,1,66,130]{3,2,1,0:T(8,128)S(1)}, f32[2,1,66,130]{3,2,1,0:T(8,128)S(1)}, u32[]{:S(2)}, u32[]{:S(2)}) collective-permute-start(f32[2,1,66,130]{3,2,1,0:T(8,128)S(1)} %get-tuple-element.136), channel_id=1, source_target_pairs={{1,0},{3,2},{5,4},{7,6},{9,8},{11,10},{13,12},{15,14},{17,16},{19,... | collective-permute-start | bytes 205928 | tf_op jit(solution)/shard_map/ppermute | solution.py:20
  89.0 37.7 %collective-permute-start.17 = (f32[2,1,66,130]{3,2,1,0:T(8,128)S(1)}, f32[2,1,66,130]{3,2,1,0:T(8,128)S(1)}, u32[]{:S(2)}, u32[]{:S(2)}) collective-permute-start(f32[2,1,66,130]{3,2,1,0:T(8,128)S(1)} %get-tuple-element.137), channel_id=1, source_target_pairs={{0,1},{2,3},{4,5},{6,7},{8,9},{10,11},{12,13},{14,15},{16,17},{18,... | collective-permute-start | bytes 205928 | tf_op jit(solution)/shard_map/ppermute | solution.py:19
  127.0 32.5 %collective-permute-start.18 = (f32[2,2,1,128]{3,2,1,0:T(1,128)S(1)}, f32[2,2,1,128]{3,2,1,0:T(1,128)S(1)}, u32[]{:S(2)}, u32[]{:S(2)}) collective-permute-start(f32[2,2,1,128]{3,2,1,0:T(1,128)S(1)} %get-tuple-element.194), channel_id=1, source_target_pairs={{0,16},{16,32},{32,48},{48,64},{64,80},{80,96},{96,112},{112,128},... | collective-permute-start | bytes 6152 | tf_op jit(solution)/shard_map/ppermute | solution.py:19
  128.8 30.7 %collective-permute-start.19 = (f32[2,2,1,128]{3,2,1,0:T(1,128)S(1)}, f32[2,2,1,128]{3,2,1,0:T(1,128)S(1)}, u32[]{:S(2)}, u32[]{:S(2)}) collective-permute-start(f32[2,2,1,128]{3,2,1,0:T(1,128)S(1)} %get-tuple-element.195), channel_id=1, source_target_pairs={{16,0},{32,16},{48,32},{64,48},{80,64},{96,80},{112,96},{128,112},... | collective-permute-start | bytes 6152 | tf_op jit(solution)/shard_map/ppermute | solution.py:20
  378.1 10.9 %collective-permute-start.30 = (f32[2,2,1,128]{3,2,1,0:T(1,128)S(1)}, f32[2,2,1,128]{3,2,1,0:T(1,128)S(1)}, u32[]{:S(2)}, u32[]{:S(2)}) collective-permute-start(f32[2,2,1,128]{3,2,1,0:T(1,128)S(1)} %get-tuple-element.188), channel_id=1, source_target_pairs={{0,16},{16,32},{32,48},{48,64},{64,80},{80,96},{96,112},{112,128},... | collective-permute-start | bytes 6152 | tf_op jit(solution)/shard_map/ppermute | solution.py:19
  382.8 12.7 %collective-permute-start.42 = (f32[2,2,1,128]{3,2,1,0:T(1,128)S(1)}, f32[2,2,1,128]{3,2,1,0:T(1,128)S(1)}, u32[]{:S(2)}, u32[]{:S(2)}) collective-permute-start(f32[2,2,1,128]{3,2,1,0:T(1,128)S(1)} %get-tuple-element.192), channel_id=1, source_target_pairs={{0,16},{16,32},{32,48},{48,64},{64,80},{80,96},{96,112},{112,128},... | collective-permute-start | bytes 6152 | tf_op jit(solution)/shard_map/ppermute | solution.py:19
  387.7 7.8 collective-permute-start.43
  400.3 9.9 %collective-permute-start.34 = (f32[2,1,66,130]{3,2,1,0:T(8,128)S(1)}, f32[2,1,66,130]{3,2,1,0:T(8,128)S(1)}, u32[]{:S(2)}, u32[]{:S(2)}) collective-permute-start(f32[2,1,66,130]{3,2,1,0:T(8,128)S(1)} %get-tuple-element.128), channel_id=1, source_target_pairs={{1,0},{3,2},{5,4},{7,6},{9,8},{11,10},{13,12},{15,14},{17,16},{19,... | collective-permute-start | bytes 205928 | tf_op jit(solution)/shard_map/ppermute | solution.py:20
  401.6 8.6 %collective-permute-start.35 = (f32[2,1,66,130]{3,2,1,0:T(8,128)S(1)}, f32[2,1,66,130]{3,2,1,0:T(8,128)S(1)}, u32[]{:S(2)}, u32[]{:S(2)}) collective-permute-start(f32[2,1,66,130]{3,2,1,0:T(8,128)S(1)} %get-tuple-element.129), channel_id=1, source_target_pairs={{0,1},{2,3},{4,5},{6,7},{8,9},{10,11},{12,13},{14,15},{16,17},{18,... | collective-permute-start | bytes 205928 | tf_op jit(solution)/shard_map/ppermute | solution.py:19
  405.8 11.1 %collective-permute-start.44 = (f32[2,2,66,1]{3,2,1,0:T(8,128)S(1)}, f32[2,2,66,1]{3,2,1,0:T(8,128)S(1)}, u32[]{:S(2)}, u32[]{:S(2)}) collective-permute-start(f32[2,2,66,1]{3,2,1,0:T(8,128)S(1)} %get-tuple-element.163), channel_id=1, source_target_pairs={{0,2},{2,4},{4,6},{6,8},{8,10},{10,12},{12,14},{1,3},{3,5},{5,7},{... | collective-permute-start | bytes 3176 | tf_op jit(solution)/shard_map/ppermute | solution.py:19
  408.0 8.9 %collective-permute-start.45 = (f32[2,2,66,1]{3,2,1,0:T(8,128)S(1)}, f32[2,2,66,1]{3,2,1,0:T(8,128)S(1)}, u32[]{:S(2)}, u32[]{:S(2)}) collective-permute-start(f32[2,2,66,1]{3,2,1,0:T(8,128)S(1)} %get-tuple-element.162), channel_id=1, source_target_pairs={{2,0},{4,2},{6,4},{8,6},{10,8},{12,10},{14,12},{3,1},{5,3},{7,5},{... | collective-permute-start | bytes 3176 | tf_op jit(solution)/shard_map/ppermute | solution.py:20
  422.1 12.0 %collective-permute-start.38 = (f32[2,2,66,1]{3,2,1,0:T(8,128)S(1)}, f32[2,2,66,1]{3,2,1,0:T(8,128)S(1)}, u32[]{:S(2)}, u32[]{:S(2)}) collective-permute-start(f32[2,2,66,1]{3,2,1,0:T(8,128)S(1)} %get-tuple-element.157), channel_id=1, source_target_pairs={{0,2},{2,4},{4,6},{6,8},{8,10},{10,12},{12,14},{1,3},{3,5},{5,7},{... | collective-permute-start | bytes 3176 | tf_op jit(solution)/shard_map/ppermute | solution.py:19
  428.9 10.9 %collective-permute-start.46 = (f32[2,1,66,130]{3,2,1,0:T(8,128)S(1)}, f32[2,1,66,130]{3,2,1,0:T(8,128)S(1)}, u32[]{:S(2)}, u32[]{:S(2)}) collective-permute-start(f32[2,1,66,130]{3,2,1,0:T(8,128)S(1)} %get-tuple-element.132), channel_id=1, source_target_pairs={{1,0},{3,2},{5,4},{7,6},{9,8},{11,10},{13,12},{15,14},{17,16},{19,... | collective-permute-start | bytes 205928 | tf_op jit(solution)/shard_map/ppermute | solution.py:20
  430.2 9.6 %collective-permute-start.47 = (f32[2,1,66,130]{3,2,1,0:T(8,128)S(1)}, f32[2,1,66,130]{3,2,1,0:T(8,128)S(1)}, u32[]{:S(2)}, u32[]{:S(2)}) collective-permute-start(f32[2,1,66,130]{3,2,1,0:T(8,128)S(1)} %get-tuple-element.133), channel_id=1, source_target_pairs={{0,1},{2,3},{4,5},{6,7},{8,9},{10,11},{12,13},{14,15},{16,17},{18,... | collective-permute-start | bytes 205928 | tf_op jit(solution)/shard_map/ppermute | solution.py:19
  453.4 10.4 %collective-permute-start.50 = (f32[2,2,66,1]{3,2,1,0:T(8,128)S(1)}, f32[2,2,66,1]{3,2,1,0:T(8,128)S(1)}, u32[]{:S(2)}, u32[]{:S(2)}) collective-permute-start(f32[2,2,66,1]{3,2,1,0:T(8,128)S(1)} %get-tuple-element.155), channel_id=1, source_target_pairs={{0,2},{2,4},{4,6},{6,8},{8,10},{10,12},{12,14},{1,3},{3,5},{5,7},{... | collective-permute-start | bytes 3176 | tf_op jit(solution)/shard_map/ppermute | solution.py:19
  485.4 13.4 %collective-permute-start.56 = (f32[2,2,66,1]{3,2,1,0:T(8,128)S(1)}, f32[2,2,66,1]{3,2,1,0:T(8,128)S(1)}, u32[]{:S(2)}, u32[]{:S(2)}) collective-permute-start(f32[2,2,66,1]{3,2,1,0:T(8,128)S(1)} %get-tuple-element.153), channel_id=1, source_target_pairs={{0,2},{2,4},{4,6},{6,8},{8,10},{10,12},{12,14},{1,3},{3,5},{5,7},{... | collective-permute-start | bytes 3176 | tf_op jit(solution)/shard_map/ppermute | solution.py:19
  489.8 9.0 %collective-permute-start.57 = (f32[2,2,66,1]{3,2,1,0:T(8,128)S(1)}, f32[2,2,66,1]{3,2,1,0:T(8,128)S(1)}, u32[]{:S(2)}, u32[]{:S(2)}) collective-permute-start(f32[2,2,66,1]{3,2,1,0:T(8,128)S(1)} %get-tuple-element.152), channel_id=1, source_target_pairs={{2,0},{4,2},{6,4},{8,6},{10,8},{12,10},{14,12},{3,1},{5,3},{7,5},{... | collective-permute-start | bytes 3176 | tf_op jit(solution)/shard_map/ppermute | solution.py:20
  491.8 12.7 %collective-permute-start.66 = (f32[2,2,1,128]{3,2,1,0:T(1,128)S(1)}, f32[2,2,1,128]{3,2,1,0:T(1,128)S(1)}, u32[]{:S(2)}, u32[]{:S(2)}) collective-permute-start(f32[2,2,1,128]{3,2,1,0:T(1,128)S(1)} %get-tuple-element.178), channel_id=1, source_target_pairs={{0,16},{16,32},{32,48},{48,64},{64,80},{80,96},{96,112},{112,128},... | collective-permute-start | bytes 6152 | tf_op jit(solution)/shard_map/ppermute | solution.py:19
  506.9 13.9 %collective-permute-start.60 = (f32[2,2,1,128]{3,2,1,0:T(1,128)S(1)}, f32[2,2,1,128]{3,2,1,0:T(1,128)S(1)}, u32[]{:S(2)}, u32[]{:S(2)}) collective-permute-start(f32[2,2,1,128]{3,2,1,0:T(1,128)S(1)} %get-tuple-element.180), channel_id=1, source_target_pairs={{0,16},{16,32},{32,48},{48,64},{64,80},{80,96},{96,112},{112,128},... | collective-permute-start | bytes 6152 | tf_op jit(solution)/shard_map/ppermute | solution.py:19
  511.8 9.1 %collective-permute-start.61 = (f32[2,2,1,128]{3,2,1,0:T(1,128)S(1)}, f32[2,2,1,128]{3,2,1,0:T(1,128)S(1)}, u32[]{:S(2)}, u32[]{:S(2)}) collective-permute-start(f32[2,2,1,128]{3,2,1,0:T(1,128)S(1)} %get-tuple-element.181), channel_id=1, source_target_pairs={{16,0},{32,16},{48,32},{64,48},{80,64},{96,80},{112,96},{128,112},... | collective-permute-start | bytes 6152 | tf_op jit(solution)/shard_map/ppermute | solution.py:20
  513.2 13.4 %collective-permute-start.68 = (f32[2,2,66,1]{3,2,1,0:T(8,128)S(1)}, f32[2,2,66,1]{3,2,1,0:T(8,128)S(1)}, u32[]{:S(2)}, u32[]{:S(2)}) collective-permute-start(f32[2,2,66,1]{3,2,1,0:T(8,128)S(1)} %get-tuple-element.149), channel_id=1, source_target_pairs={{0,2},{2,4},{4,6},{6,8},{8,10},{10,12},{12,14},{1,3},{3,5},{5,7},{... | collective-permute-start | bytes 3176 | tf_op jit(solution)/shard_map/ppermute | solution.py:19
  518.9 7.7 collective-permute-start.69
  531.3 10.8 %collective-permute-start.64 = (f32[2,1,66,130]{3,2,1,0:T(8,128)S(1)}, f32[2,1,66,130]{3,2,1,0:T(8,128)S(1)}, u32[]{:S(2)}, u32[]{:S(2)}) collective-permute-start(f32[2,1,66,130]{3,2,1,0:T(8,128)S(1)} %get-tuple-element.120), channel_id=1, source_target_pairs={{1,0},{3,2},{5,4},{7,6},{9,8},{11,10},{13,12},{15,14},{17,16},{19,... | collective-permute-start | bytes 205928 | tf_op jit(solution)/shard_map/ppermute | solution.py:20
  532.6 9.5 %collective-permute-start.65 = (f32[2,1,66,130]{3,2,1,0:T(8,128)S(1)}, f32[2,1,66,130]{3,2,1,0:T(8,128)S(1)}, u32[]{:S(2)}, u32[]{:S(2)}) collective-permute-start(f32[2,1,66,130]{3,2,1,0:T(8,128)S(1)} %get-tuple-element.121), channel_id=1, source_target_pairs={{0,1},{2,3},{4,5},{6,7},{8,9},{10,11},{12,13},{14,15},{16,17},{18,... | collective-permute-start | bytes 205928 | tf_op jit(solution)/shard_map/ppermute | solution.py:19
  536.8 170.1 %collective-permute-start.70 = (f32[2,1,66,130]{3,2,1,0:T(8,128)S(1)}, f32[2,1,66,130]{3,2,1,0:T(8,128)S(1)}, u32[]{:S(2)}, u32[]{:S(2)}) collective-permute-start(f32[2,1,66,130]{3,2,1,0:T(8,128)S(1)} %get-tuple-element.118), channel_id=1, source_target_pairs={{1,0},{3,2},{5,4},{7,6},{9,8},{11,10},{13,12},{15,14},{17,16},{19,... | collective-permute-start | bytes 205928 | tf_op jit(solution)/shard_map/ppermute | solution.py:20
  538.1 168.8 %collective-permute-start.71 = (f32[2,1,66,130]{3,2,1,0:T(8,128)S(1)}, f32[2,1,66,130]{3,2,1,0:T(8,128)S(1)}, u32[]{:S(2)}, u32[]{:S(2)}) collective-permute-start(f32[2,1,66,130]{3,2,1,0:T(8,128)S(1)} %get-tuple-element.119), channel_id=1, source_target_pairs={{0,1},{2,3},{4,5},{6,7},{8,9},{10,11},{12,13},{14,15},{16,17},{18,... | collective-permute-start | bytes 205928 | tf_op jit(solution)/shard_map/ppermute | solution.py:19
  716.2 7.7 collective-permute-start.74
  744.1 7.7 collective-permute-start.80
  772.4 7.7 collective-permute-start.86
  (62 other events, 655.1 us)
where the time goes:
time: 796 us; the launch traced here: 793 us
  blocking collectives  317 us (40%)
  starting transfers between devices  269 us (34%)
  waiting for transfers between devices  102 us (13%)
  matrix products  44.2 us (6%)
  local copies, waits for them, and re-layouts  33.9 us (4%)
  other arithmetic  24.6 us (3%)
    ppermute x45, starting transfers between devices, extended(): before = lax.ppermute(last, axis, up)  194 us
    psum x2, blocking collectives, fk_round(): whole_sums = lax.psum(partial_sums, ('col', 'gz'))  158 us
    all_gather x2, blocking collectives, fk_round(): lax.all_gather(trace, 'row', axis=1, tiled=True)  96 us
    ppermute x45, waiting for transfers between devices, extended(): after = lax.ppermute(leading, axis, down)  88.5 us
    ppermute x45, starting transfers between devices, extended(): after = lax.ppermute(leading, axis, down)  75.6 us
    dot_general x8, matrix products, block_sum(): lax.dot_general(piece_traces, kernel, (((1,), (1,)), ((), ())), precision...  44.2 us
    all_gather x1, blocking collectives, on_device(): lax.all_gather(jnp.concatenate([node_pos, node_weight[None, :]], 0), 'row...  33.6 us
    all_gather x1, blocking collectives, on_device(): target_pos = lax.all_gather(node_pos, ('col', 'gz'), axis=1, tiled=True)  29.4 us
  transfers between devices with their start and end apart: 90, of which 44 were waited for; matrix products, arithmetic and copies ran while one was open for 7% of the time, Pallas kernels for 0%

commit v1 on v0

--- a/solution.py
+++ b/solution.py
@@ -85,7 +85,8 @@
         first = relax_all(first, forcing)
         trace = jnp.take(first.reshape(images, cell_count), owner_cell, axis=1)
         partial_sums = kernel_apply(lax.all_gather(trace, "row", axis=1, tiled=True))
-        whole_sums = lax.psum(partial_sums, ("col", "gz"))
+        parts = lax.all_gather(partial_sums, ("col", "gz"))
+        whole_sums = jnp.sum(parts, axis=0)
         summed = lax.dynamic_slice_in_dim(
             whole_sums, lax.axis_index(("col", "gz")) * node_count, node_count, 1
         )

time: 796 us -> 697 us (0.88)
  blocking collectives: 317 us -> 225 us
  starting transfers between devices: 269 us -> 259 us
    psum x2 -> x0, blocking collectives: 158 us -> none  [fk_round(): whole_sums = lax.psum(partial_sums, ('col', 'gz'))]
    all_gather x0 -> x2, blocking collectives: none -> 61.8 us  [fk_round(): parts = lax.all_gather(partial_sums, ('col', 'gz'))]
  transfers between devices with their start and end apart: 90 -> 90, of which waited for: 44 -> 43; matrix products, arithmetic and copies ran while one was open for 7% -> 7% of each run, Pallas kernels for 0% -> 0%
where the time goes in v1:
time: 697 us; the launch traced here: 694 us
  starting transfers between devices  259 us (37%)
  blocking collectives  225 us (32%)
  waiting for transfers between devices  105 us (15%)
  matrix products  44.2 us (6%)
  local copies, waits for them, and re-layouts  33.3 us (5%)
  other arithmetic  24.7 us (4%)
    ppermute x45, starting transfers between devices, extended(): before = lax.ppermute(last, axis, up)  186 us
    all_gather x2, blocking collectives, fk_round(): lax.all_gather(trace, 'row', axis=1, tiled=True)  99.9 us
    ppermute x45, waiting for transfers between devices, extended(): after = lax.ppermute(leading, axis, down)  91 us
    ppermute x45, starting transfers between devices, extended(): after = lax.ppermute(leading, axis, down)  73.5 us
    all_gather x2, blocking collectives, fk_round(): parts = lax.all_gather(partial_sums, ('col', 'gz'))  61.8 us
    dot_general x8, matrix products, block_sum(): lax.dot_general(piece_traces, kernel, (((1,), (1,)), ((), ())), precision...  44.2 us
    all_gather x1, blocking collectives, on_device(): lax.all_gather(jnp.concatenate([node_pos, node_weight[None, :]], 0), 'row...  33.6 us
    all_gather x1, blocking collectives, on_device(): target_pos = lax.all_gather(node_pos, ('col', 'gz'), axis=1, tiled=True)  29.4 us
  transfers between devices with their start and end apart: 90, of which 43 were waited for; matrix products, arithmetic and copies ran while one was open for 7% of the time, Pallas kernels for 0%

profile of v1, /device:TPU:1, one launch (start us, length us, event | category | flops | bytes accessed | tf_op | source)
XLA Modules:
  0.0 694.1 jit_solution(7293898002494712638)
XLA Ops:
  0.7 5.8 collective-permute-start
  7.8 5.8 collective-permute-done.1
  13.8 5.0 collective-permute-start.2
  30.7 6.0 broadcast_multiply_fusion
  37.9 5.7 collective-permute-start.6
  75.6 5.4 collective-permute-start.14
  93.1 33.6 %all_gather.18 = f32[4,2048]{1,0:T(4,128)S(1)} all-gather(f32[4,128]{1,0:T(4,128)S(1)} %pad_maximum_fusion.298), channel_id=1, replica_groups=mesh['row'=16,'col'=8,'gz'=2] {'row'}, dimensions={1}, use_global_device_ids=true | all-gather | bytes 34816 | tf_op jit(solution)/shard_map/all_gather | solution.py:58
  130.1 29.4 %all_gather.19 = f32[3,2048]{1,0:T(4,128)S(1)} all-gather(f32[3,128]{1,0:T(4,128)S(1)} %copy-done.1), channel_id=1, replica_groups=mesh['row'=16,'col'=8,'gz'=2] {'col','gz'}, dimensions={1}, use_global_device_ids=true | all-gather | bytes 26112 | tf_op jit(solution)/shard_map/all_gather | solution.py:57
  184.9 50.7 %all_gather.20 = f32[2,2048]{0,1:T(8,128)S(1)} all-gather(f32[2,128]{0,1:T(8,128)S(1)} %select_bitcast_fusion.1), channel_id=1, replica_groups=mesh['row'=16,'col'=8,'gz'=2] {'row'}, dimensions={1}, use_global_device_ids=true | all-gather | bytes 17408 | tf_op jit(solution)/shard_map/all_gather | solution.py:87
  236.0 22.4 %while.20 = (s32[]{:T(128)}, f32[4,2,512]{2,1,0:T(2,128)S(1)}, f32[4,2048]{1,0:T(4,128)S(1)}, f32[4,3,512]{2,1,0:T(4,128)S(1)}, f32[2,2048]{1,0:T(2,128)S(1)}, /*index=5*/s32[]{:T(128)}, s32[]{:T(128)}, s32[]{}, s32[]{}) while((s32[]{:T(128)}, f32[4,2,512]{2,1,0:T(2,128)S(1)}, f32[4,2048]{1,0:T(4,128)S(1)}, f32[4,3,512]{2,1,0:T(4,128)S(1)}, ...), condition=%wide.region_1.3_spmd, body=%wide.region_0.2_spmd.sunk | while | flops 38797316 | bytes 137349 | solution.py:81
  236.0 5.5 fusion.245
  241.6 5.5 fusion.245
  247.2 5.5 fusion.245
  252.8 5.5 fusion.245
  258.4 33.2 %all_gather.21 = f32[16,2,2048]{2,1,0:T(2,128)S(1)} all-gather(f32[1,2,2048]{2,1,0:T(2,128)S(1)} %bitcast.114), channel_id=1, replica_groups=mesh['row'=16,'col'=8,'gz'=2] {'col','gz'}, dimensions={0}, use_global_device_ids=true | all-gather | bytes 278528 | tf_op jit(solution)/shard_map/all_gather | solution.py:88
  291.8 4.9 scatter_custom_fusion
  296.7 5.2 copy.37
  361.3 5.8 collective-permute-start.36
  368.6 5.3 collective-permute-done.37
  394.1 5.5 collective-permute-start.48
  405.0 6.8 collective-permute-start.50
  435.4 5.1 collective-permute-start.56
  442.5 5.7 collective-permute-start.66
  463.9 5.5 collective-permute-start.68
  501.7 49.2 %all_gather.22 = f32[2,2048]{0,1:T(8,128)S(1)} all-gather(f32[2,128]{0,1:T(8,128)S(1)} %select_bitcast_fusion), channel_id=1, replica_groups=mesh['row'=16,'col'=8,'gz'=2] {'row'}, dimensions={1}, use_global_device_ids=true | all-gather | bytes 17408 | tf_op jit(solution)/shard_map/all_gather | solution.py:87
  551.2 22.4 %while.21 = (s32[]{:T(128)}, f32[4,2,512]{2,1,0:T(2,128)S(1)}, f32[4,2048]{1,0:T(4,128)S(1)}, f32[4,3,512]{2,1,0:T(4,128)S(1)}, f32[2,2048]{1,0:T(2,128)S(1)}, /*index=5*/s32[]{:T(128)}, s32[]{:T(128)}, s32[]{}, s32[]{}) while((s32[]{:T(128)}, f32[4,2,512]{2,1,0:T(2,128)S(1)}, f32[4,2048]{1,0:T(4,128)S(1)}, f32[4,3,512]{2,1,0:T(4,128)S(1)}, ...), condition=%wide.region_5.7_spmd, body=%wide.region_4.6_spmd.sunk | while | flops 38797316 | bytes 137349 | solution.py:81
  551.3 5.5 fusion.248
  556.9 5.5 fusion.248
  562.5 5.5 fusion.248
  568.1 5.5 fusion.248
  573.6 28.6 %all_gather.23 = f32[16,2,2048]{2,1,0:T(2,128)S(1)} all-gather(f32[1,2,2048]{2,1,0:T(2,128)S(1)} %bitcast.115), channel_id=1, replica_groups=mesh['row'=16,'col'=8,'gz'=2] {'col','gz'}, dimensions={0}, use_global_device_ids=true | all-gather | bytes 278528 | tf_op jit(solution)/shard_map/all_gather | solution.py:88
  607.4 5.2 copy.44
  (307 shorter events, 333.8 us)
Async XLA Ops:
  13.8 8.5 %collective-permute-start.2 = (f32[2,2,66,1]{3,2,1,0:T(8,128)S(1)}, f32[2,2,66,1]{3,2,1,0:T(8,128)S(1)}, u32[]{:S(2)}, u32[]{:S(2)}) collective-permute-start(f32[2,2,66,1]{3,2,1,0:T(8,128)S(1)} %get-tuple-element.195), channel_id=1, source_target_pairs={{0,2},{2,4},{4,6},{6,8},{8,10},{10,12},{12,14},{1,3},{3,5},{5,7},{... | collective-permute-start | bytes 3176 | tf_op jit(solution)/shard_map/ppermute | solution.py:19
  25.4 11.3 %collective-permute-start.4 = (f32[2,1,66,130]{3,2,1,0:T(8,128)S(1)}, f32[2,1,66,130]{3,2,1,0:T(8,128)S(1)}, u32[]{:S(2)}, u32[]{:S(2)}) collective-permute-start(f32[2,1,66,130]{3,2,1,0:T(8,128)S(1)} %get-tuple-element.164), channel_id=1, source_target_pairs={{1,0},{3,2},{5,4},{7,6},{9,8},{11,10},{13,12},{15,14},{17,16},{19,... | collective-permute-start | bytes 205928 | tf_op jit(solution)/shard_map/ppermute | solution.py:20
  26.7 10.0 %collective-permute-start.5 = (f32[2,1,66,130]{3,2,1,0:T(8,128)S(1)}, f32[2,1,66,130]{3,2,1,0:T(8,128)S(1)}, u32[]{:S(2)}, u32[]{:S(2)}) collective-permute-start(f32[2,1,66,130]{3,2,1,0:T(8,128)S(1)} %get-tuple-element.165), channel_id=1, source_target_pairs={{0,1},{2,3},{4,5},{6,7},{8,9},{10,11},{12,13},{14,15},{16,17},{18,... | collective-permute-start | bytes 205928 | tf_op jit(solution)/shard_map/ppermute | solution.py:19
  75.6 7.5 %collective-permute-start.14 = (f32[2,2,66,1]{3,2,1,0:T(8,128)S(1)}, f32[2,2,66,1]{3,2,1,0:T(8,128)S(1)}, u32[]{:S(2)}, u32[]{:S(2)}) collective-permute-start(f32[2,2,66,1]{3,2,1,0:T(8,128)S(1)} %get-tuple-element.191), channel_id=1, source_target_pairs={{0,2},{2,4},{4,6},{6,8},{8,10},{10,12},{12,14},{1,3},{3,5},{5,7},{... | collective-permute-start | bytes 3176 | tf_op jit(solution)/shard_map/ppermute | solution.py:19
  87.7 39.0 %collective-permute-start.16 = (f32[2,1,66,130]{3,2,1,0:T(8,128)S(1)}, f32[2,1,66,130]{3,2,1,0:T(8,128)S(1)}, u32[]{:S(2)}, u32[]{:S(2)}) collective-permute-start(f32[2,1,66,130]{3,2,1,0:T(8,128)S(1)} %get-tuple-element.160), channel_id=1, source_target_pairs={{1,0},{3,2},{5,4},{7,6},{9,8},{11,10},{13,12},{15,14},{17,16},{19,... | collective-permute-start | bytes 205928 | tf_op jit(solution)/shard_map/ppermute | solution.py:20
  89.0 37.7 %collective-permute-start.17 = (f32[2,1,66,130]{3,2,1,0:T(8,128)S(1)}, f32[2,1,66,130]{3,2,1,0:T(8,128)S(1)}, u32[]{:S(2)}, u32[]{:S(2)}) collective-permute-start(f32[2,1,66,130]{3,2,1,0:T(8,128)S(1)} %get-tuple-element.161), channel_id=1, source_target_pairs={{0,1},{2,3},{4,5},{6,7},{8,9},{10,11},{12,13},{14,15},{16,17},{18,... | collective-permute-start | bytes 205928 | tf_op jit(solution)/shard_map/ppermute | solution.py:19
  127.0 32.5 %collective-permute-start.18 = (f32[2,2,1,128]{3,2,1,0:T(1,128)S(1)}, f32[2,2,1,128]{3,2,1,0:T(1,128)S(1)}, u32[]{:S(2)}, u32[]{:S(2)}) collective-permute-start(f32[2,2,1,128]{3,2,1,0:T(1,128)S(1)} %get-tuple-element.218), channel_id=1, source_target_pairs={{0,16},{16,32},{32,48},{48,64},{64,80},{80,96},{96,112},{112,128},... | collective-permute-start | bytes 6152 | tf_op jit(solution)/shard_map/ppermute | solution.py:19
  128.8 30.7 %collective-permute-start.19 = (f32[2,2,1,128]{3,2,1,0:T(1,128)S(1)}, f32[2,2,1,128]{3,2,1,0:T(1,128)S(1)}, u32[]{:S(2)}, u32[]{:S(2)}) collective-permute-start(f32[2,2,1,128]{3,2,1,0:T(1,128)S(1)} %get-tuple-element.219), channel_id=1, source_target_pairs={{16,0},{32,16},{48,32},{64,48},{80,64},{96,80},{112,96},{128,112},... | collective-permute-start | bytes 6152 | tf_op jit(solution)/shard_map/ppermute | solution.py:20
  330.5 10.4 %collective-permute-start.30 = (f32[2,2,1,128]{3,2,1,0:T(1,128)S(1)}, f32[2,2,1,128]{3,2,1,0:T(1,128)S(1)}, u32[]{:S(2)}, u32[]{:S(2)}) collective-permute-start(f32[2,2,1,128]{3,2,1,0:T(1,128)S(1)} %get-tuple-element.212), channel_id=1, source_target_pairs={{0,16},{16,32},{32,48},{48,64},{64,80},{80,96},{96,112},{112,128},... | collective-permute-start | bytes 6152 | tf_op jit(solution)/shard_map/ppermute | solution.py:19
  333.4 7.5 %collective-permute-start.31 = (f32[2,2,1,128]{3,2,1,0:T(1,128)S(1)}, f32[2,2,1,128]{3,2,1,0:T(1,128)S(1)}, u32[]{:S(2)}, u32[]{:S(2)}) collective-permute-start(f32[2,2,1,128]{3,2,1,0:T(1,128)S(1)} %get-tuple-element.213), channel_id=1, source_target_pairs={{16,0},{32,16},{48,32},{64,48},{80,64},{96,80},{112,96},{128,112},... | collective-permute-start | bytes 6152 | tf_op jit(solution)/shard_map/ppermute | solution.py:20
  334.7 11.7 %collective-permute-start.42 = (f32[2,2,1,128]{3,2,1,0:T(1,128)S(1)}, f32[2,2,1,128]{3,2,1,0:T(1,128)S(1)}, u32[]{:S(2)}, u32[]{:S(2)}) collective-permute-start(f32[2,2,1,128]{3,2,1,0:T(1,128)S(1)} %get-tuple-element.216), channel_id=1, source_target_pairs={{0,16},{16,32},{32,48},{48,64},{64,80},{80,96},{96,112},{112,128},... | collective-permute-start | bytes 6152 | tf_op jit(solution)/shard_map/ppermute | solution.py:19
  351.1 9.9 %collective-permute-start.34 = (f32[2,1,66,130]{3,2,1,0:T(8,128)S(1)}, f32[2,1,66,130]{3,2,1,0:T(8,128)S(1)}, u32[]{:S(2)}, u32[]{:S(2)}) collective-permute-start(f32[2,1,66,130]{3,2,1,0:T(8,128)S(1)} %get-tuple-element.152), channel_id=1, source_target_pairs={{1,0},{3,2},{5,4},{7,6},{9,8},{11,10},{13,12},{15,14},{17,16},{19,... | collective-permute-start | bytes 205928 | tf_op jit(solution)/shard_map/ppermute | solution.py:20
  352.4 8.6 %collective-permute-start.35 = (f32[2,1,66,130]{3,2,1,0:T(8,128)S(1)}, f32[2,1,66,130]{3,2,1,0:T(8,128)S(1)}, u32[]{:S(2)}, u32[]{:S(2)}) collective-permute-start(f32[2,1,66,130]{3,2,1,0:T(8,128)S(1)} %get-tuple-element.153), channel_id=1, source_target_pairs={{0,1},{2,3},{4,5},{6,7},{8,9},{10,11},{12,13},{14,15},{16,17},{18,... | collective-permute-start | bytes 205928 | tf_op jit(solution)/shard_map/ppermute | solution.py:19
  356.6 11.7 %collective-permute-start.44 = (f32[2,2,66,1]{3,2,1,0:T(8,128)S(1)}, f32[2,2,66,1]{3,2,1,0:T(8,128)S(1)}, u32[]{:S(2)}, u32[]{:S(2)}) collective-permute-start(f32[2,2,66,1]{3,2,1,0:T(8,128)S(1)} %get-tuple-element.187), channel_id=1, source_target_pairs={{0,2},{2,4},{4,6},{6,8},{8,10},{10,12},{12,14},{1,3},{3,5},{5,7},{... | collective-permute-start | bytes 3176 | tf_op jit(solution)/shard_map/ppermute | solution.py:19
  358.9 9.5 %collective-permute-start.45 = (f32[2,2,66,1]{3,2,1,0:T(8,128)S(1)}, f32[2,2,66,1]{3,2,1,0:T(8,128)S(1)}, u32[]{:S(2)}, u32[]{:S(2)}) collective-permute-start(f32[2,2,66,1]{3,2,1,0:T(8,128)S(1)} %get-tuple-element.186), channel_id=1, source_target_pairs={{2,0},{4,2},{6,4},{8,6},{10,8},{12,10},{14,12},{3,1},{5,3},{7,5},{... | collective-permute-start | bytes 3176 | tf_op jit(solution)/shard_map/ppermute | solution.py:20
  374.1 11.7 %collective-permute-start.38 = (f32[2,2,66,1]{3,2,1,0:T(8,128)S(1)}, f32[2,2,66,1]{3,2,1,0:T(8,128)S(1)}, u32[]{:S(2)}, u32[]{:S(2)}) collective-permute-start(f32[2,2,66,1]{3,2,1,0:T(8,128)S(1)} %get-tuple-element.181), channel_id=1, source_target_pairs={{0,2},{2,4},{4,6},{6,8},{8,10},{10,12},{12,14},{1,3},{3,5},{5,7},{... | collective-permute-start | bytes 3176 | tf_op jit(solution)/shard_map/ppermute | solution.py:19
  380.5 10.9 %collective-permute-start.46 = (f32[2,1,66,130]{3,2,1,0:T(8,128)S(1)}, f32[2,1,66,130]{3,2,1,0:T(8,128)S(1)}, u32[]{:S(2)}, u32[]{:S(2)}) collective-permute-start(f32[2,1,66,130]{3,2,1,0:T(8,128)S(1)} %get-tuple-element.156), channel_id=1, source_target_pairs={{1,0},{3,2},{5,4},{7,6},{9,8},{11,10},{13,12},{15,14},{17,16},{19,... | collective-permute-start | bytes 205928 | tf_op jit(solution)/shard_map/ppermute | solution.py:20
  381.8 9.6 %collective-permute-start.47 = (f32[2,1,66,130]{3,2,1,0:T(8,128)S(1)}, f32[2,1,66,130]{3,2,1,0:T(8,128)S(1)}, u32[]{:S(2)}, u32[]{:S(2)}) collective-permute-start(f32[2,1,66,130]{3,2,1,0:T(8,128)S(1)} %get-tuple-element.157), channel_id=1, source_target_pairs={{0,1},{2,3},{4,5},{6,7},{8,9},{10,11},{12,13},{14,15},{16,17},{18,... | collective-permute-start | bytes 205928 | tf_op jit(solution)/shard_map/ppermute | solution.py:19
  405.0 8.9 %collective-permute-start.50 = (f32[2,2,66,1]{3,2,1,0:T(8,128)S(1)}, f32[2,2,66,1]{3,2,1,0:T(8,128)S(1)}, u32[]{:S(2)}, u32[]{:S(2)}) collective-permute-start(f32[2,2,66,1]{3,2,1,0:T(8,128)S(1)} %get-tuple-element.179), channel_id=1, source_target_pairs={{0,2},{2,4},{4,6},{6,8},{8,10},{10,12},{12,14},{1,3},{3,5},{5,7},{... | collective-permute-start | bytes 3176 | tf_op jit(solution)/shard_map/ppermute | solution.py:19
  435.4 14.1 %collective-permute-start.56 = (f32[2,2,66,1]{3,2,1,0:T(8,128)S(1)}, f32[2,2,66,1]{3,2,1,0:T(8,128)S(1)}, u32[]{:S(2)}, u32[]{:S(2)}) collective-permute-start(f32[2,2,66,1]{3,2,1,0:T(8,128)S(1)} %get-tuple-element.177), channel_id=1, source_target_pairs={{0,2},{2,4},{4,6},{6,8},{8,10},{10,12},{12,14},{1,3},{3,5},{5,7},{... | collective-permute-start | bytes 3176 | tf_op jit(solution)/shard_map/ppermute | solution.py:19
  440.6 9.0 %collective-permute-start.57 = (f32[2,2,66,1]{3,2,1,0:T(8,128)S(1)}, f32[2,2,66,1]{3,2,1,0:T(8,128)S(1)}, u32[]{:S(2)}, u32[]{:S(2)}) collective-permute-start(f32[2,2,66,1]{3,2,1,0:T(8,128)S(1)} %get-tuple-element.176), channel_id=1, source_target_pairs={{2,0},{4,2},{6,4},{8,6},{10,8},{12,10},{14,12},{3,1},{5,3},{7,5},{... | collective-permute-start | bytes 3176 | tf_op jit(solution)/shard_map/ppermute | solution.py:20
  442.5 12.7 %collective-permute-start.66 = (f32[2,2,1,128]{3,2,1,0:T(1,128)S(1)}, f32[2,2,1,128]{3,2,1,0:T(1,128)S(1)}, u32[]{:S(2)}, u32[]{:S(2)}) collective-permute-start(f32[2,2,1,128]{3,2,1,0:T(1,128)S(1)} %get-tuple-element.202), channel_id=1, source_target_pairs={{0,16},{16,32},{32,48},{48,64},{64,80},{80,96},{96,112},{112,128},... | collective-permute-start | bytes 6152 | tf_op jit(solution)/shard_map/ppermute | solution.py:19
  457.6 13.7 %collective-permute-start.60 = (f32[2,2,1,128]{3,2,1,0:T(1,128)S(1)}, f32[2,2,1,128]{3,2,1,0:T(1,128)S(1)}, u32[]{:S(2)}, u32[]{:S(2)}) collective-permute-start(f32[2,2,1,128]{3,2,1,0:T(1,128)S(1)} %get-tuple-element.204), channel_id=1, source_target_pairs={{0,16},{16,32},{32,48},{48,64},{64,80},{80,96},{96,112},{112,128},... | collective-permute-start | bytes 6152 | tf_op jit(solution)/shard_map/ppermute | solution.py:19
  462.5 8.8 %collective-permute-start.61 = (f32[2,2,1,128]{3,2,1,0:T(1,128)S(1)}, f32[2,2,1,128]{3,2,1,0:T(1,128)S(1)}, u32[]{:S(2)}, u32[]{:S(2)}) collective-permute-start(f32[2,2,1,128]{3,2,1,0:T(1,128)S(1)} %get-tuple-element.205), channel_id=1, source_target_pairs={{16,0},{32,16},{48,32},{64,48},{80,64},{96,80},{112,96},{128,112},... | collective-permute-start | bytes 6152 | tf_op jit(solution)/shard_map/ppermute | solution.py:20
  463.9 13.2 %collective-permute-start.68 = (f32[2,2,66,1]{3,2,1,0:T(8,128)S(1)}, f32[2,2,66,1]{3,2,1,0:T(8,128)S(1)}, u32[]{:S(2)}, u32[]{:S(2)}) collective-permute-start(f32[2,2,66,1]{3,2,1,0:T(8,128)S(1)} %get-tuple-element.173), channel_id=1, source_target_pairs={{0,2},{2,4},{4,6},{6,8},{8,10},{10,12},{12,14},{1,3},{3,5},{5,7},{... | collective-permute-start | bytes 3176 | tf_op jit(solution)/shard_map/ppermute | solution.py:19
  469.4 7.7 %collective-permute-start.69 = (f32[2,2,66,1]{3,2,1,0:T(8,128)S(1)}, f32[2,2,66,1]{3,2,1,0:T(8,128)S(1)}, u32[]{:S(2)}, u32[]{:S(2)}) collective-permute-start(f32[2,2,66,1]{3,2,1,0:T(8,128)S(1)} %get-tuple-element.172), channel_id=1, source_target_pairs={{2,0},{4,2},{6,4},{8,6},{10,8},{12,10},{14,12},{3,1},{5,3},{7,5},{... | collective-permute-start | bytes 3176 | tf_op jit(solution)/shard_map/ppermute | solution.py:20
  481.8 10.8 %collective-permute-start.64 = (f32[2,1,66,130]{3,2,1,0:T(8,128)S(1)}, f32[2,1,66,130]{3,2,1,0:T(8,128)S(1)}, u32[]{:S(2)}, u32[]{:S(2)}) collective-permute-start(f32[2,1,66,130]{3,2,1,0:T(8,128)S(1)} %get-tuple-element.144), channel_id=1, source_target_pairs={{1,0},{3,2},{5,4},{7,6},{9,8},{11,10},{13,12},{15,14},{17,16},{19,... | collective-permute-start | bytes 205928 | tf_op jit(solution)/shard_map/ppermute | solution.py:20
  483.1 9.5 %collective-permute-start.65 = (f32[2,1,66,130]{3,2,1,0:T(8,128)S(1)}, f32[2,1,66,130]{3,2,1,0:T(8,128)S(1)}, u32[]{:S(2)}, u32[]{:S(2)}) collective-permute-start(f32[2,1,66,130]{3,2,1,0:T(8,128)S(1)} %get-tuple-element.145), channel_id=1, source_target_pairs={{0,1},{2,3},{4,5},{6,7},{8,9},{10,11},{12,13},{14,15},{16,17},{18,... | collective-permute-start | bytes 205928 | tf_op jit(solution)/shard_map/ppermute | solution.py:19
  487.3 125.3 %collective-permute-start.70 = (f32[2,1,66,130]{3,2,1,0:T(8,128)S(1)}, f32[2,1,66,130]{3,2,1,0:T(8,128)S(1)}, u32[]{:S(2)}, u32[]{:S(2)}) collective-permute-start(f32[2,1,66,130]{3,2,1,0:T(8,128)S(1)} %get-tuple-element.142), channel_id=1, source_target_pairs={{1,0},{3,2},{5,4},{7,6},{9,8},{11,10},{13,12},{15,14},{17,16},{19,... | collective-permute-start | bytes 205928 | tf_op jit(solution)/shard_map/ppermute | solution.py:20
  488.6 124.0 %collective-permute-start.71 = (f32[2,1,66,130]{3,2,1,0:T(8,128)S(1)}, f32[2,1,66,130]{3,2,1,0:T(8,128)S(1)}, u32[]{:S(2)}, u32[]{:S(2)}) collective-permute-start(f32[2,1,66,130]{3,2,1,0:T(8,128)S(1)} %get-tuple-element.143), channel_id=1, source_target_pairs={{0,1},{2,3},{4,5},{6,7},{8,9},{10,11},{12,13},{14,15},{16,17},{18,... | collective-permute-start | bytes 205928 | tf_op jit(solution)/shard_map/ppermute | solution.py:19
  631.6 7.7 %collective-permute-start.76 = (f32[2,1,66,130]{3,2,1,0:T(8,128)S(1)}, f32[2,1,66,130]{3,2,1,0:T(8,128)S(1)}, u32[]{:S(2)}, u32[]{:S(2)}) collective-permute-start(f32[2,1,66,130]{3,2,1,0:T(8,128)S(1)} %get-tuple-element.140), channel_id=1, source_target_pairs={{1,0},{3,2},{5,4},{7,6},{9,8},{11,10},{13,12},{15,14},{17,16},{19,... | collective-permute-start | bytes 205928 | tf_op jit(solution)/shard_map/ppermute | solution.py:20
  632.9 7.3 %collective-permute-start.77 = (f32[2,1,66,130]{3,2,1,0:T(8,128)S(1)}, f32[2,1,66,130]{3,2,1,0:T(8,128)S(1)}, u32[]{:S(2)}, u32[]{:S(2)}) collective-permute-start(f32[2,1,66,130]{3,2,1,0:T(8,128)S(1)} %get-tuple-element.141), channel_id=1, source_target_pairs={{0,1},{2,3},{4,5},{6,7},{8,9},{10,11},{12,13},{14,15},{16,17},{18,... | collective-permute-start | bytes 205928 | tf_op jit(solution)/shard_map/ppermute | solution.py:19
  (62 other events, 648.0 us)
